TPU v7x, 32 devices: a whole 2x2x4 slice. The times are simulated.
32 devices in a mesh: group: 1, expert: 16 (over z, y, x), dp: 2 (over core).
Axes of the slice: x: 2, y: 2, z: 4, core: 2. Of those that a mesh axis runs over, the one named last changes fastest.
Arguments:
- tokens: bfloat16 [2048, 4096], P(('group', 'expert', 'dp')), may hold values from -6 to 6
- queries: bfloat16 [2048, 4096], P(('group', 'expert', 'dp')), may hold values from -6 to 6
- keys_local: bfloat16 [2048, 256], P(('group', 'expert', 'dp')), may hold values from -6 to 6
- values_local: bfloat16 [2048, 256], P(('group', 'expert', 'dp')), may hold values from -6 to 6
- prompt_keys: bfloat16 [1024, 256], P('group'), may hold values from -6 to 6
- prompt_values: bfloat16 [1024, 256], P('group'), may hold values from -6 to 6
- norm_gain: float32 [4096], replicated, may hold values from 0.25 to 1.75
- expert_ids: int32 [2048, 8], P(('group', 'expert', 'dp')), may hold values from 0 to 15, all different within a row; in each aligned block of 64 rows (0 to 63, 64 to 127, ...) at most 42 rows name the same one
- route_weight: float32 [2048, 8], P(('group', 'expert', 'dp')), may hold values from 0.05 to 1
- stored_gate: bfloat16 [16, 4096, 768], P('expert', None, 'dp'), may hold values from -0.09375 to 0.09375
- stored_up: bfloat16 [16, 4096, 768], P('expert', None, 'dp'), may hold values from -0.09375 to 0.09375
- stored_down: bfloat16 [16, 768, 4096], P('expert', 'dp'), may hold values from -0.21875 to 0.21875
- holder: int32 [16], replicated, may hold values from 0 to 15, as said below
Outputs:
- layer_out: bfloat16 [2048, 4096], P(('group', 'expert', 'dp'))
Inputs may be any that keep to these rules, and one draw needn't show every extreme that they name: `expert_ids`: each row names 8 different experts. In the 64 rows of one device no expert is named more than 42 times, and in every draw some expert is named exactly 42 times in some device's rows. holder[s] is s or the slot 8 away (s + 16 / 2 modulo 16), holder[holder[s]] = s, and holder[0] = 8.
All inputs are finite; a program needn't handle non-finite values.
Results may differ from a plain program's by a relative error of at most 0.0055.
Values may be sent and summed in bfloat16 or wider, within the bound.
A program may use at most 192 MiB of HBM per device.

v0:
```python
import jax
import jax.numpy as jnp
from jax import lax
from jax.sharding import PartitionSpec as P

HEADS = 32
KVH = 2
HD = 128
TOPK = 8
EXP_DEV = 1
PREFIX = 1024


def attend_rows(queries, keys_local, values_local, prompt_keys, prompt_values):
    count_rows = queries.shape[0]
    grouping = HEADS // KVH
    query_all = queries.reshape(count_rows, KVH, grouping, HD)
    key_all = jnp.concatenate([prompt_keys, keys_local], 0).reshape(-1, KVH, HD)
    value_all = jnp.concatenate([prompt_values, values_local], 0).reshape(-1, KVH, HD)
    scores = jnp.einsum(
        "tkgd,skd->kgts", query_all, key_all, preferred_element_type=jnp.float32
    ) * HD ** (-0.5)
    column = jnp.arange(key_all.shape[0], dtype=jnp.int32)
    row_index = jnp.arange(count_rows, dtype=jnp.int32)
    allowed = (column[None, :] < PREFIX) | (column[None, :] - PREFIX <= row_index[:, None])
    scores = jnp.where(allowed[None, None], scores, -jnp.inf)
    highest = jnp.max(scores, axis=-1, keepdims=True)
    expons = jnp.exp(scores - highest)
    weights = (expons / jnp.sum(expons, axis=-1, keepdims=True)).astype(jnp.bfloat16)
    context = jnp.einsum("kgts,skd->tkgd", weights, value_all, preferred_element_type=jnp.float32)
    return context.reshape(count_rows, HEADS * HD)


def expert_rows(picked, gate_w, up_w, down_w):
    gate_val = jnp.dot(picked, gate_w, preferred_element_type=jnp.float32)
    up_val = jnp.dot(picked, up_w, preferred_element_type=jnp.float32)
    hidden = (jax.nn.silu(gate_val) * up_val).astype(jnp.bfloat16)
    return jnp.dot(hidden, down_w, preferred_element_type=jnp.float32).astype(jnp.bfloat16)


def local(
    tokens,
    queries,
    keys_local,
    values_local,
    prompt_keys,
    prompt_values,
    norm_gain,
    expert_ids,
    route_weight,
    stored_gate,
    stored_up,
    stored_down,
    holder,
):
    owners = lax.axis_size("expert")
    tok_count = tokens.shape[0]
    model_width = tokens.shape[1]
    capacity = min(tok_count, max(2, tok_count * TOPK * 4 // (3 * owners * EXP_DEV)))
    gate_w = stored_gate[0]
    up_w = stored_up[0]
    down_w = stored_down[0]
    context = attend_rows(queries, keys_local, values_local, prompt_keys, prompt_values)
    widened = tokens.astype(jnp.float32)
    normed = (
        widened * lax.rsqrt(jnp.mean(widened * widened, axis=-1, keepdims=True) + 1e-06) * norm_gain
    ).astype(jnp.bfloat16)
    shares = route_weight / jnp.sum(route_weight, axis=-1, keepdims=True)
    flat_ids = expert_ids.reshape(-1)
    onehot = (flat_ids[:, None] == jnp.arange(owners, dtype=jnp.int32)[None, :]).astype(jnp.int32)
    earlier = jnp.cumsum(onehot, axis=0) - onehot
    slot_of = jnp.sum(earlier * onehot, axis=1)
    places = (holder[flat_ids] * capacity + slot_of).reshape(tok_count, TOPK)
    chooser = (
        (jnp.arange(owners * capacity, dtype=jnp.int32)[:, None, None] == places[None])
        .any(axis=2)
        .astype(jnp.bfloat16)
    )
    send_rows = (
        jnp.dot(chooser, normed, preferred_element_type=jnp.float32)
        .astype(jnp.bfloat16)
        .reshape(owners, capacity, model_width)
    )
    both_rows = lax.all_gather(
        lax.all_to_all(send_rows, "expert", split_axis=0, concat_axis=0, tiled=True)[None],
        "dp",
        axis=0,
        tiled=True,
    )
    partial_out = expert_rows(both_rows.reshape(-1, model_width), gate_w, up_w, down_w)
    partial_out = partial_out.astype(jnp.float32).reshape(both_rows.shape)
    own_sum = lax.psum_scatter(
        partial_out.astype(jnp.bfloat16), "dp", scatter_dimension=0, tiled=True
    ).astype(jnp.float32)[0]
    results = lax.all_to_all(
        own_sum.astype(jnp.bfloat16), "expert", split_axis=0, concat_axis=0, tiled=True
    )
    gathered = results.reshape(owners * capacity, model_width)[places]
    mixture = jnp.einsum("tk,tkd->td", shares, gathered.astype(jnp.float32))
    return (widened + context + mixture).astype(jnp.bfloat16)


def solution(mesh):
    return jax.shard_map(
        local,
        mesh=mesh,
        in_specs=(
            P(("group", "expert", "dp"), None),
            P(("group", "expert", "dp"), None),
            P(("group", "expert", "dp"), None),
            P(("group", "expert", "dp"), None),
            P("group", None),
            P("group", None),
            P(),
            P(("group", "expert", "dp"), None),
            P(("group", "expert", "dp"), None),
            P("expert", None, "dp"),
            P("expert", None, "dp"),
            P("expert", "dp", None),
            P(),
        ),
        out_specs=P(("group", "expert", "dp"), None),
        check_vma=False,
    )
```

profile of v0, /device:TPU:14, one launch (start us, length us, event | category | flops | bytes accessed | tf_op | source)
XLA Modules:
  0.0 474.5 jit_solution(1100816948195221598)
XLA Ops:
  6.5 0.0 copy-start
  6.5 0.0 all-gather.3.cloned.1.call-start
  6.5 0.9 copy.43
  7.5 0.1 reshape.181
  7.6 0.1 eq.43
  7.6 0.1 eq.39
  7.7 2.0 fusion.56
  9.7 4.4 compare_select_fusion.2
  14.1 0.1 compare_reduce_fusion.8
  14.2 1.2 reduce-window.6
  15.3 0.2 slice_reduce_fusion
  15.6 0.1 fusion.46
  15.7 5.6 %fusion.48 = s32[512]{0:T(512)S(1)} fusion(s32[512]{0:T(512)S(1)} %fusion.46, pred[512]{0:T(512)(128)(4,1)S(1)} %get-tuple-element.13, pred[512]{0:T(512)(128)(4,1)S(1)} %get-tuple-element.12, pred[512]{0:T(512)(128)(4,1)S(1)} %get-tuple-element.11, pred[512]{0:T(512)(128)(4,1)S(1)} %get-tuple-element.10, pred[512]{0:T(512)(128)(4,1)S(1)} %get-tuple-element.9, ...), kind=kLoop, calls=%fused_computation.76 | loop fusion | flops 5632 | bytes 10788 | tf_op jit(solution)/shard_map/add | solution.py:73
  21.3 0.1 add.80
  21.4 0.5 fusion.20
  21.9 1.2 fusion.26
  23.2 5.2 %convolution_convert_fusion.1 = bf16[672,4096]{1,0:T(8,128)(2,1)} fusion(pred[672,64]{0,1:T(8,128)(4,1)S(1)} %fusion.20, bf16[64,4096]{1,0:T(8,128)(2,1)} %param.13, f32[4096]{0:T(1024)} %param.19, f32[64]{0:T(128)S(1)} %add_rsqrt_fusion), kind=kOutput, calls=%fused_computation.7 | convolution fusion | flops 356122624 | bytes 6088960 | tf_op jit(solution)/shard_map/dot_general | solution.py:80
  28.3 6.2 %reshape.183 = bf16[16,42,4096]{2,1,0:T(8,128)(2,1)} reshape(bf16[672,4096]{1,0:T(8,128)(2,1)} %convolution_convert_fusion.1) | data formatting | bytes 11010048 | tf_op jit(solution)/shard_map/reshape | solution.py:82
  34.5 143.7 %all_to_all.10 = bf16[16,42,4096]{2,1,0:T(8,128)(2,1)S(1)} all-to-all(bf16[16,42,4096]{2,1,0:T(8,128)(2,1)} %reshape.183), channel_id=1, replica_groups=mesh['group'=1,'expert'=16,'dp'=2] {'expert'}, dimensions={0} | all-to-all | bytes 11010048 | tf_op jit(solution)/shard_map/all_to_all | solution.py:85
  178.3 5.4 %copy.47 = bf16[16,42,4096]{2,0,1:T(8,128)(2,1)} copy(bf16[16,42,4096]{2,1,0:T(8,128)(2,1)S(1)} %all_to_all.10) | data formatting | bytes 11010048 | tf_op jit(solution)/shard_map/all_to_all | solution.py:85
  183.7 0.0 all-gather.3.cloned.1.call-update
  183.7 0.2 reduce-scatter.2.cloned.1.call-start
  183.9 23.3 %all-gather.3.cloned.1.call-done = bf16[32,42,4096]{2,0,1:T(8,128)(2,1)} async-done(((bf16[16,42,4096]{2,0,1:T(8,128)(2,1)}), bf16[32,42,4096]{2,0,1:T(8,128)(2,1)}) %all-gather.3.cloned.1.call-update) | async-done | bytes 11010064 | tf_op jit(solution)/shard_map/all_gather | solution.py:84
  207.3 14.0 %copy.48 = bf16[32,42,4096]{2,1,0:T(8,128)(2,1)} copy(bf16[32,42,4096]{2,0,1:T(8,128)(2,1)} %all-gather.3.cloned.1.call-done) | data formatting | bytes 22020096 | tf_op jit(solution)/shard_map/all_gather | solution.py:84
  221.3 11.9 %reshape.184 = bf16[1344,4096]{1,0:T(8,128)(2,1)} reshape(bf16[32,42,4096]{2,1,0:T(8,128)(2,1)} %copy.48) | data formatting | bytes 22020096 | tf_op jit(solution)/shard_map/reshape | solution.py:90
  233.2 10.5 %fusion.10 = f32[1344,384]{1,0:T(8,128)} fusion(bf16[1344,4096]{1,0:T(8,128)(2,1)} %reshape.184, bf16[1,4096,384]{2,1,0:T(8,128)(2,1)} %param.22), kind=kOutput, calls=%fused_computation.17 | convolution fusion | flops 4227858432 | bytes 16220160 | tf_op jit(solution)/shard_map/dot_general | solution.py:35
  243.7 0.0 copy-done
  243.7 17.9 %convolution_convert_fusion = bf16[1344,4096]{1,0:T(8,128)(2,1)} fusion(bf16[1,384,4096]{2,1,0:T(8,128)(2,1)S(1)} %copy-done, bf16[1344,4096]{1,0:T(8,128)(2,1)} %reshape.184, bf16[1,4096,384]{2,1,0:T(8,128)(2,1)} %param.23, f32[1344,384]{1,0:T(8,128)} %fusion.10), kind=kOutput, calls=%fused_computation.2 | convolution fusion | flops 8464318464 | bytes 30375936 | tf_op jit(solution)/shard_map/dot_general | solution.py:38
  261.6 11.7 %convert_element_type.48 = bf16[2,16,42,4096]{3,2,1,0:T(8,128)(2,1)} reshape(bf16[1344,4096]{1,0:T(8,128)(2,1)} %convolution_convert_fusion) | data formatting | bytes 22020096 | tf_op jit(solution)/shard_map/convert_element_type | solution.py:93
  273.3 0.0 reduce-scatter.2.cloned.1.call-update
  273.4 23.3 %reduce-scatter.2.cloned.1.call-done = bf16[1,16,42,4096]{3,2,1,0:T(8,128)(2,1)} async-done(((bf16[2,16,42,4096]{3,2,1,0:T(8,128)(2,1)}), bf16[1,16,42,4096]{3,2,1,0:T(8,128)(2,1)}) %reduce-scatter.2.cloned.1.call-update) | async-done | bytes 5505040 | tf_op jit(solution)/shard_map/reduce_scatter | solution.py:92
  296.6 0.0 copy-start.4
  296.6 0.0 copy-start.7
  296.6 0.0 copy-start.5
  296.6 0.0 copy-start.6
  296.7 0.0 copy-start.8
  296.7 7.1 %all-to-all-start.1 = ((bf16[16,42,4096]{2,1,0:T(8,128)(2,1)}), bf16[16,42,4096]{2,1,0:T(8,128)(2,1)}, u32[]{:S(2)}, u32[]{:S(2)}) async-start(bf16[16,42,4096]{2,1,0:T(8,128)(2,1)} %bitcast.96), calls=%async_computation.2 | async-start | bytes 12582912 | tf_op jit(solution)/shard_map/all_to_all | solution.py:95
  303.8 0.1 add.84
  303.9 0.1 reshape.211
  304.0 0.0 copy-done.9
  304.0 0.1 copy.51
  304.1 0.0 copy-done.4
  304.1 0.0 copy-done.7
  304.2 0.3 copy.38
  304.5 0.0 copy-done.5
  304.5 0.9 copy.58
  305.4 0.0 copy-done.6
  305.4 0.0 copy-done.8
  305.4 0.3 copy.37
  305.7 0.1 fusion.39
  305.8 4.3 fusion.57
  310.1 5.9 %fusion.21 = f32[64,2,16,128]{3,0,2,1:T(8,128)S(1)} fusion(bf16[1088,2,128,1]{0,2,3,1:T(8,128)(2,1)S(1)} %bitcast.100, f32[2,16,64]{2,1,0:T(8,128)S(1)} %fusion.57, pred[64,1088]{1,0:T(8,128)(4,1)S(1)} %fusion.39, bf16[1088,2,128,1]{0,2,3,1:T(8,128)(2,1)S(1)} %bitcast.99, bf16[64,2,16,128]{3,2,1,0:T(8,128)(2,1)} %bitcast.103), kind=kOutput, calls=%fused_computation.28 | convolution fusion | flops 1151994880 | bytes 2764800 | tf_op jit(solution)/shard_map/kgts,skd->tkgd/dot_general | solution.py:30
  316.0 1.6 copy.42
  317.6 126.1 %all-to-all-done.1 = bf16[16,42,4096]{2,1,0:T(8,128)(2,1)} async-done(((bf16[16,42,4096]{2,1,0:T(8,128)(2,1)}), bf16[16,42,4096]{2,1,0:T(8,128)(2,1)}, u32[]{:S(2)}, u32[]{:S(2)}) %all-to-all-start.1) | async-done | bytes 5505056 | tf_op jit(solution)/shard_map/all_to_all | solution.py:95
  443.7 6.2 %reshape.185 = bf16[672,4096]{1,0:T(8,128)(2,1)} reshape(bf16[16,42,4096]{2,1,0:T(8,128)(2,1)} %all-to-all-done.1) | data formatting | bytes 11010048 | tf_op jit(solution)/shard_map/reshape | solution.py:98
  449.9 0.0 copy-start.1
  449.9 12.2 %gather_fusion = bf16[512,4096]{1,0:T(8,128)(2,1)} fusion(bf16[672,4096]{1,0:T(8,128)(2,1)} %reshape.185, s32[1024]{0:T(1024)S(1)} %pad_clamp_fusion), kind=kCustom, calls=%fused_computation | custom fusion | bytes 8390656 | tf_op jit(solution)/shard_map/gather | solution.py:98
  462.1 0.0 copy-start.2
  462.1 0.0 copy-start.3
  462.1 3.5 fusion.6
  465.7 0.0 copy-done.2
  465.7 0.0 copy-done.3
  465.7 1.9 fusion.25
  467.6 0.0 copy-done.1
  (13 shorter events, 0.2 us)
Async XLA Ops:
  6.5 237.2 %copy-start = (bf16[1,384,4096]{2,1,0:T(8,128)(2,1)S(1)}, bf16[1,384,4096]{2,1,0:T(8,128)(2,1)}, u32[]{:S(2)}) copy-start(bf16[1,384,4096]{2,1,0:T(8,128)(2,1)} %param.24) | copy-start | bytes 9437188
  6.5 200.7 %all-gather.3.cloned.1.call-start = ((), (), s32[]{:S(2)}) async-start(), calls=%async_computation.4 | async-start | bytes 16515072 | tf_op jit(solution)/shard_map/all_gather | solution.py:84
  183.7 112.9 %reduce-scatter.2.cloned.1.call-start = ((), (), s32[]{:S(2)}) async-start(), calls=%async_computation.3 | async-start | bytes 18874368 | tf_op jit(solution)/shard_map/reduce_scatter | solution.py:92
  296.6 7.3 %copy-start.9 = (f32[64,8]{0,1:T(8,128)S(1)}, f32[64,8]{0,1:T(8,128)}, u32[]{:S(2)}) copy-start(f32[64,8]{0,1:T(8,128)} %param.21) | copy-start | bytes 6148
  296.6 7.5 %copy-start.4 = (bf16[1024,256]{1,0:T(8,128)(2,1)S(1)}, bf16[1024,256]{1,0:T(8,128)(2,1)}, u32[]{:S(2)}) copy-start(bf16[1024,256]{1,0:T(8,128)(2,1)} %param.17) | copy-start | bytes 1572868
  296.6 7.5 %copy-start.7 = (bf16[64,256]{1,0:T(8,128)(2,1)S(1)}, bf16[64,256]{1,0:T(8,128)(2,1)}, u32[]{:S(2)}) copy-start(bf16[64,256]{1,0:T(8,128)(2,1)} %param.15) | copy-start | bytes 98308
  296.6 7.8 %copy-start.5 = (bf16[64,4096]{1,0:T(8,128)(2,1)S(1)}, bf16[64,4096]{1,0:T(8,128)(2,1)}, u32[]{:S(2)}) copy-start(bf16[64,4096]{1,0:T(8,128)(2,1)} %param.14) | copy-start | bytes 1572868
  296.6 8.7 %copy-start.6 = (bf16[1024,256]{1,0:T(8,128)(2,1)S(1)}, bf16[1024,256]{1,0:T(8,128)(2,1)}, u32[]{:S(2)}) copy-start(bf16[1024,256]{1,0:T(8,128)(2,1)} %param.18) | copy-start | bytes 1572868
  296.7 8.7 %copy-start.8 = (bf16[64,256]{1,0:T(8,128)(2,1)S(1)}, bf16[64,256]{1,0:T(8,128)(2,1)}, u32[]{:S(2)}) copy-start(bf16[64,256]{1,0:T(8,128)(2,1)} %param.16) | copy-start | bytes 98308
  296.7 147.0 %all-to-all-start.1 = ((bf16[16,42,4096]{2,1,0:T(8,128)(2,1)}), bf16[16,42,4096]{2,1,0:T(8,128)(2,1)}, u32[]{:S(2)}, u32[]{:S(2)}) async-start(bf16[16,42,4096]{2,1,0:T(8,128)(2,1)} %bitcast.96), calls=%async_computation.2 | async-start | bytes 12582912 | tf_op jit(solution)/shard_map/all_to_all | solution.py:95
  449.9 17.8 %copy-start.1 = (bf16[1,384,4096]{2,1,0:T(8,128)(2,1)S(1)}, bf16[1,384,4096]{2,1,0:T(8,128)(2,1)}, u32[]{:S(2)}) copy-start(bf16[1,384,4096]{2,1,0:T(8,128)(2,1)} %param.24) | copy-start | bytes 9437188
  462.1 3.6 copy-start.2
  462.1 3.6 copy-start.3
Sparse Core Ops, SparseCore 0:
  183.8 23.3 all-gather.2
  273.5 23.1 reduce-scatter.1
where the time goes:
time: 476 us; the launch traced here: 474 us
  waiting for transfers between devices  173 us (36%)
  blocking collectives  144 us (30%)
  local copies, waits for them, and re-layouts  74.5 us (16%)
  matrix products  47.4 us (10%)
  other arithmetic  15.2 us (3%)
  between operations  13.6 us (3%)
  starting transfers between devices  7.33 us (2%)
    all_to_all x1, blocking collectives, local(): lax.all_to_all(send_rows, 'expert', split_axis=0, concat_axis=0, tiled=True)  144 us
    all_to_all x1, waiting for transfers between devices, local(): lax.all_to_all(own_sum.astype(jnp.bfloat16), 'expert', split_axis=0, conc...  126 us
    all_gather x1, waiting for transfers between devices, local(): lax.all_gather(lax.all_to_all(send_rows, 'expert', split_axis=0, concat_a...  23.3 us
    reduce_scatter x1, waiting for transfers between devices, local(): lax.psum_scatter(partial_out.astype(jnp.bfloat16), 'dp', scatter_dimensio...  23.3 us
    dot_general x1, matrix products, expert_rows(): jnp.dot(hidden, down_w, preferred_element_type=jnp.float32)  17.9 us
    all_gather x1, local copies, waits for them, and re-layouts, local(): lax.all_gather(lax.all_to_all(send_rows, 'expert', split_axis=0, concat_a...  14 us
    gather x1, local copies, waits for them, and re-layouts, local(): gathered = results.reshape(owners * capacity, model_width)[places]  12.2 us
    reshape x1, local copies, waits for them, and re-layouts, local(): both_rows.reshape(-1, model_width)  11.9 us
  transfers between devices with their start and end apart: 3, of which 3 were waited for; matrix products, arithmetic and copies ran while one was open for 3% of the time, Pallas kernels for 0%

commit v1 on v0

--- a/solution.py
+++ b/solution.py
@@ -1,6 +1,8 @@
 import jax
 import jax.numpy as jnp
 from jax import lax
+from jax.experimental import pallas as pl
+from jax.experimental.pallas import tpu as pltpu
 from jax.sharding import PartitionSpec as P
 
 HEADS = 32
@@ -38,6 +40,53 @@
     return jnp.dot(hidden, down_w, preferred_element_type=jnp.float32).astype(jnp.bfloat16)
 
 
+def ffn_body(x_ref, w_ref, gate_ref, up_ref, down_ref, out_ref):
+    rows = x_ref[...]
+    gate_val = jnp.dot(rows, gate_ref[0], preferred_element_type=jnp.float32)
+    up_val = jnp.dot(rows, up_ref[0], preferred_element_type=jnp.float32)
+    hidden = gate_val / (1.0 + jnp.exp(-gate_val)) * up_val * w_ref[...]
+    out_ref[...] = jnp.dot(
+        hidden.astype(jnp.bfloat16), down_ref[0], preferred_element_type=jnp.float32
+    ).astype(jnp.bfloat16)
+
+
+def dense_ffn(rows, scale, gate_w, up_w, down_w):
+    count, width = rows.shape[0], gate_w.shape[1]
+    tile = 256
+    return pl.pallas_call(
+        ffn_body,
+        grid=(count // tile,),
+        out_shape=jax.ShapeDtypeStruct((count, width), jnp.bfloat16),
+        in_specs=[
+            pl.BlockSpec((tile, width), lambda i: (i, 0)),
+            pl.BlockSpec((tile, 1), lambda i: (i, 0)),
+            pl.BlockSpec(gate_w.shape, lambda i: (0, 0, 0), pipeline_mode=pl.Buffered(1)),
+            pl.BlockSpec(up_w.shape, lambda i: (0, 0, 0), pipeline_mode=pl.Buffered(1)),
+            pl.BlockSpec(down_w.shape, lambda i: (0, 0, 0), pipeline_mode=pl.Buffered(1)),
+        ],
+        out_specs=pl.BlockSpec((tile, width), lambda i: (i, 0)),
+        compiler_params=pltpu.CompilerParams(
+            dimension_semantics=("arbitrary",), vmem_limit_bytes=48 * 1024 * 1024
+        ),
+    )(rows, scale, gate_w, up_w, down_w)
+
+
+def dense_mixture(normed, shares, expert_ids, gate_w, up_w, down_w, holder):
+    owners = lax.axis_size("expert")
+    axes = ("expert", "dp")
+    named = expert_ids[:, :, None] == jnp.arange(owners, dtype=jnp.int32)[None, None, :]
+    table = jnp.sum(jnp.where(named, shares[:, :, None], 0.0), axis=1)
+    high = table.astype(jnp.bfloat16)
+    low = (table - high.astype(jnp.float32)).astype(jnp.bfloat16)
+    spread = lax.all_gather(jnp.concatenate([high, low], axis=1), axes, axis=0, tiled=True)
+    rows = lax.all_gather(normed, axes, axis=0, tiled=True)
+    mine = holder[lax.axis_index("expert")]
+    pick = jnp.arange(2 * owners, dtype=jnp.int32) % owners == mine
+    scale = jnp.sum(jnp.where(pick[None], spread.astype(jnp.float32), 0.0), axis=1, keepdims=True)
+    partial_out = dense_ffn(rows, scale, gate_w, up_w, down_w)
+    return lax.psum_scatter(partial_out, axes, scatter_dimension=0, tiled=True).astype(jnp.float32)
+
+
 def local(
     tokens,
     queries,
@@ -66,6 +115,12 @@
         widened * lax.rsqrt(jnp.mean(widened * widened, axis=-1, keepdims=True) + 1e-06) * norm_gain
     ).astype(jnp.bfloat16)
     shares = route_weight / jnp.sum(route_weight, axis=-1, keepdims=True)
+    devices = owners * lax.axis_size("dp")
+    if devices * tok_count <= 2 * lax.axis_size("dp") * owners * capacity:
+        mixture = dense_mixture(
+            normed, shares, expert_ids, stored_gate, stored_up, stored_down, holder
+        )
+        return (widened + context + mixture).astype(jnp.bfloat16)
     flat_ids = expert_ids.reshape(-1)
     onehot = (flat_ids[:, None] == jnp.arange(owners, dtype=jnp.int32)[None, :]).astype(jnp.int32)
     earlier = jnp.cumsum(onehot, axis=0) - onehot

time: 476 us -> 354 us (0.74)
  blocking collectives: 144 us -> 30.5 us
  waiting for transfers between devices: 173 us -> 253 us
  local copies, waits for them, and re-layouts: 74.5 us -> 6.06 us
  matrix products: 47.4 us -> 8.54 us
  Pallas kernels: 0 us -> 33.1 us
  starting transfers between devices: 7.33 us -> 0.04 us
  other arithmetic: 15.2 us -> 8.69 us
    reduce_scatter x1, waiting for transfers between devices: 23.3 us -> 174 us  [dense_mixture(): lax.psum_scatter(partial_out, axes, scatter_dimension=0, tiled=True)]
    all_to_all x1 -> x0, blocking collectives: 144 us -> none  [local(): lax.all_to_all(send_rows, 'expert', split_axis=0, concat_axis=0, tiled=True)]
    all_to_all x1 -> x0, waiting for transfers between devices: 126 us -> none  [local(): lax.all_to_all(own_sum.astype(jnp.bfloat16), 'expert', split_axis=0, conc...]
    all_gather x1, waiting for transfers between devices: 23.3 us -> 79.6 us  [dense_mixture(): rows = lax.all_gather(normed, axes, axis=0, tiled=True)]
    dot_general x4 -> x0, matrix products: 37.2 us -> none  [the longest x1 17.9 us: expert_rows(): jnp.dot(hidden, down_w, preferred_element_type=jnp.float32)]
    pallas_call x0 -> x1, Pallas kernels: none -> 33.1 us  [dense_ffn(): pl.pallas_call(ffn_body, grid=(count // tile,), out_shape=jax.ShapeDtypeS...]
    all_gather x0 -> x1, blocking collectives: none -> 30.5 us  [dense_mixture(): lax.all_gather(jnp.concatenate([high, low], axis=1), axes, axis=0, tiled=...]
    reshape x4 -> x0, local copies, waits for them, and re-layouts: 24.3 us -> none  [the longest x1 11.9 us: local(): both_rows.reshape(-1, model_width)]
  transfers between devices with their start and end apart: 3 -> 2, of which waited for: 3 -> 2; matrix products, arithmetic and copies ran while one was open for 3% -> 4% of each run, Pallas kernels for 0% -> 0%
where the time goes in v1:
time: 354 us
  waiting for transfers between devices  253 us (71%)
  Pallas kernels  33.1 us (9%)
  blocking collectives  30.5 us (9%)
  between operations  13.6 us (4%)
  other arithmetic  8.69 us (2%)
  matrix products  8.54 us (2%)
  local copies, waits for them, and re-layouts  6.06 us (2%)
    reduce_scatter x1, waiting for transfers between devices, dense_mixture(): lax.psum_scatter(partial_out, axes, scatter_dimension=0, tiled=True)  174 us
    all_gather x1, waiting for transfers between devices, dense_mixture(): rows = lax.all_gather(normed, axes, axis=0, tiled=True)  79.6 us
    pallas_call x1, Pallas kernels, dense_ffn(): pl.pallas_call(ffn_body, grid=(count // tile,), out_shape=jax.ShapeDtypeS...  33.1 us
    all_gather x1, blocking collectives, dense_mixture(): lax.all_gather(jnp.concatenate([high, low], axis=1), axes, axis=0, tiled=...  30.5 us
  transfers between devices with their start and end apart: 2, of which 2 were waited for; matrix products, arithmetic and copies ran while one was open for 4% of the time, Pallas kernels for 0%

profile of v1, /device:TPU:14, one launch (start us, length us, event | category | flops | bytes accessed | tf_op | source)
XLA Modules:
  0.0 353.8 jit_solution(7599875951745467530)
XLA Ops:
  6.5 0.0 all-gather.3.cloned.1.call-start
  6.5 1.2 fusion.11
  7.8 2.0 fusion.13
  9.8 0.0 all-gather.3.cloned.1.call-update
  9.9 0.0 reduce-scatter.2.cloned.1.call-start
  9.9 0.7 reduce_sum.47
  10.6 0.7 broadcast_divide_fusion
  11.3 0.7 select_reduce_fusion.1
  12.0 30.5 %all-gather = bf16[32,64,32]{1,2,0:T(8,128)(2,1)S(1)} all-gather(bf16[1,64,32]{1,2,0:T(8,128)(2,1)S(1)} %maximum_bitcast_fusion), channel_id=1, replica_groups=mesh['group'=1,'expert'=16,'dp'=2] {'expert','dp'}, dimensions={0}, use_global_device_ids=true | all-gather | bytes 135168 | tf_op jit(solution)/shard_map/all_gather | solution.py:81
  42.6 0.1 copy.52
  42.7 0.2 reshape.87
  42.9 1.2 dynamic_slice.3
  44.1 0.6 fusion.25
  44.7 0.1 select_reduce_fusion
  44.8 0.4 copy.53.w_ref
  45.1 79.6 %all-gather.3.cloned.1.call-done.x_ref = bf16[2048,4096]{1,0:T(8,128)(2,1)} async-done(((bf16[64,4096]{1,0:T(8,128)(2,1)}), bf16[2048,4096]{1,0:T(8,128)(2,1)}) %all-gather.3.cloned.1.call-update) | async-done | bytes 16777232 | tf_op jit(solution)/shard_map/all_gather | solution.py:82
  124.7 0.0 copy-start
  124.7 1.9 copy-done
  126.6 33.1 %shard_map.127 = bf16[2048,4096]{1,0:T(8,128)(2,1)} custom-call(bf16[2048,4096]{1,0:T(8,128)(2,1)} %all-gather.3.cloned.1.call-done.x_ref, f32[2048,1]{1,0:T(8,128)S(1)} %copy.53.w_ref, bf16[1,4096,384]{2,1,0:T(8,128)(2,1)S(1)} %copy-done, bf16[1,4096,384]{2,1,0:T(8,128)(2,1)} %up_ref.1, bf16[1,384,4096]{2,1,0:T(8,128)(2,1)} %down_ref.1), custom_call_target="tpu_custom_call" | custom-call | tf_op jit(solution)/shard_map/pallas_call | solution.py:56
  159.7 0.0 copy-start.2
  159.7 0.0 copy-start.5
  159.7 0.0 copy-start.3
  159.7 0.0 copy-start.4
  159.7 0.0 copy-start.6
  159.7 0.0 reduce-scatter.2.cloned.1.call-update
  159.7 1.0 copy-done.2
  160.7 0.0 copy-done.5
  160.8 0.3 copy.47
  161.1 0.0 copy-done.3
  161.1 0.1 copy.60
  161.2 0.0 copy-done.4
  161.2 0.0 copy-done.6
  161.2 0.3 copy.46
  161.5 0.1 fusion.20
  161.6 3.7 %fusion.32 = f32[2,16,64]{2,1,0:T(8,128)S(1)} fusion(pred[64,1088]{1,0:T(8,128)(4,1)S(1)} %fusion.20, bf16[1088,2,128,1]{0,2,3,1:T(8,128)(2,1)S(1)} %bitcast.40, bf16[64,2,16,128]{3,2,1,0:T(8,128)(2,1)S(1)} %bitcast.44), kind=kOutput, calls=%fused_computation.41 | convolution fusion | flops 579339328 | bytes 1159168 | tf_op jit(solution)/shard_map/sub | solution.py:30
  165.3 0.0 copy-start.1
  165.3 4.9 %fusion.6 = f32[64,2,16,128]{3,0,2,1:T(8,128)S(1)} fusion(bf16[1088,2,128,1]{0,2,3,1:T(8,128)(2,1)S(1)} %bitcast.42, f32[2,16,64]{2,1,0:T(8,128)S(1)} %fusion.32, pred[64,1088]{1,0:T(8,128)(4,1)S(1)} %fusion.20, bf16[1088,2,128,1]{0,2,3,1:T(8,128)(2,1)S(1)} %bitcast.41, bf16[64,2,16,128]{3,2,1,0:T(8,128)(2,1)S(1)} %bitcast.45), kind=kOutput, calls=%fused_computation.12 | convolution fusion | flops 1151994880 | bytes 2764800 | tf_op jit(solution)/shard_map/kgts,skd->tkgd/dot_general | solution.py:32
  170.2 0.6 copy.51
  170.8 173.7 %reduce-scatter.2.cloned.1.call-done = bf16[64,4096]{1,0:T(8,128)(2,1)} async-done(((bf16[2048,4096]{1,0:T(8,128)(2,1)}), bf16[64,4096]{1,0:T(8,128)(2,1)}) %reduce-scatter.2.cloned.1.call-update) | async-done | bytes 524304 | tf_op jit(solution)/shard_map/reduce_scatter | solution.py:87
  344.5 0.0 copy-done.1
  344.5 2.5 fusion.10
  (7 shorter events, 0.1 us)
Async XLA Ops:
  6.5 118.2 %all-gather.3.cloned.1.call-start = ((), (), s32[]{:S(2)}) async-start(), calls=%async_computation.1 | async-start | bytes 17301504 | tf_op jit(solution)/shard_map/all_gather | solution.py:82
  9.9 334.6 %reduce-scatter.2.cloned.1.call-start = ((), (), s32[]{:S(2)}) async-start(), calls=%async_computation.2 | async-start | bytes 17301504 | tf_op jit(solution)/shard_map/reduce_scatter | solution.py:87
  124.7 1.9 copy-start
  159.7 1.0 copy-start.2
  159.7 1.0 copy-start.5
  159.7 1.4 copy-start.3
  159.7 1.5 copy-start.4
  159.7 1.5 copy-start.6
  165.3 179.2 %copy-start.1 = (bf16[64,4096]{1,0:T(8,128)(2,1)S(1)}, bf16[64,4096]{1,0:T(8,128)(2,1)}, u32[]{:S(2)}) copy-start(bf16[64,4096]{1,0:T(8,128)(2,1)} %param.13) | copy-start | bytes 1572868
Sparse Core Ops, SparseCore 0:
  10.2 114.4 all-gather.2
  159.8 184.5 reduce-scatter.1
